TPU v7x, 512 devices: a whole 4x4x16 slice. The times are simulated.
512 devices in a mesh: gx: 128 (over x_lo, z, y), gy: 4 (over x_hi, core).
Axes of the slice: x: 4 (x_hi: 2, x_lo: 2; x = x_hi * 2 + x_lo), y: 4, z: 16, core: 2. Of those that a mesh axis runs over, the one named last changes fastest.
Arguments:
- populations: float32 [19, 1024, 64, 128], P(None, 'gx', 'gy'), as said below
- order_field: float32 [1024, 64, 128], P('gx', 'gy'), may hold values from -1 to 1
- solid_flags: int32 [1024, 64, 128], P('gx', 'gy'), may hold values 0 or 1
- plane_flags: int32 [128], replicated, may hold values 0 or 1
- shear_shift: int32 [1], replicated, may hold values from 1 to 63
- link_site: int32 [524288], P(('gx', 'gy')), may hold values from 0 to 16383, as said below
- link_dir: int32 [524288], P(('gx', 'gy')), may hold values from 1 to 18
- link_colloid: int32 [524288], P(('gx', 'gy')), may hold values from 0 to 2047
- link_count: int32 [4096], P(('gx', 'gy')), may hold values from 1 to 128, 327680 in all
- colloid_slot: int32 [2048], replicated, may hold values from 0 to 2047, each once
- colloid_speed: float32 [3, 2048], replicated, may hold values from -0.6 to 0.6
Outputs:
- new_populations: float32 [19, 1024, 64, 128], P(None, 'gx', 'gy')
- new_order: float32 [1024, 64, 128], P('gx', 'gy')
- colloid_force: float32 [3, 2048], P(None, ('gx', 'gy'))
Inputs may be any that keep to these rules, and one draw needn't show every extreme that they name: `populations`: populations lie between 0.2 w_i and 1.8 w_i. `link_site`: the slots of one device name distinct sites in rising order, one in each run of (8 * 16 * 128) / 1024 sites.
All inputs are finite; a program needn't handle non-finite values. No bound on the sum of `solid_flags` or of `link_count` on one device may be relied on, other than what follows from the above.
Results may differ from a plain program's by a relative error of at most 0.00002.
Values sent between devices are 32-bit elements; how exact they have to be, the bound alone decides.
A program may use at most 64 MiB of HBM per device.

v0:
```python
import jax
import jax.numpy as jnp
from jax import lax
from jax.sharding import PartitionSpec as P

VELOCITIES = [
    [0, 0, 0],
    [1, 0, 0],
    [-1, 0, 0],
    [0, 1, 0],
    [0, -1, 0],
    [0, 0, 1],
    [0, 0, -1],
    [1, 1, 0],
    [-1, -1, 0],
    [1, -1, 0],
    [-1, 1, 0],
    [1, 0, 1],
    [-1, 0, -1],
    [1, 0, -1],
    [-1, 0, 1],
    [0, 1, 1],
    [0, -1, -1],
    [0, 1, -1],
    [0, -1, 1],
]
WEIGHTS = [1.0 / 3.0] + [1.0 / 18.0] * 6 + [1.0 / 36.0] * 12
OPPOSITE = [0, 2, 1, 4, 3, 6, 5, 8, 7, 10, 9, 12, 11, 14, 13, 16, 15, 18, 17]
UP_X = [1, 7, 9, 11, 13]
DOWN_X = [2, 8, 10, 12, 14]
UP_Y = [3, 7, 10, 15, 17]
DOWN_Y = [4, 8, 9, 16, 18]
TAU = 0.8
BULK = 0.04
KAPPA = 0.04
MOBILITY = 0.2
PLANE_SPEED = 0.05


def padded_2(block, sides, width):
    for axis, dim in sides:
        count = lax.axis_size(axis)
        forward = [(i, i + 1) for i in range(count - 1)]
        forward.append((count - 1, 0))
        backward = [(target, source) for source, target in forward]
        low = lax.ppermute(
            lax.slice_in_dim(block, block.shape[dim] - width, None, axis=dim), axis, forward
        )
        high = lax.ppermute(lax.slice_in_dim(block, 0, width, axis=dim), axis, backward)
        block = jnp.concatenate([low, block, high], axis=dim)
    return block


def moments(stack):
    velocity_table = jnp.array(VELOCITIES, jnp.float32)
    shape = (19,) + (1,) * (stack.ndim - 1)
    density = jnp.sum(stack, axis=0)
    speed_x = jnp.sum(stack * velocity_table[:, 0].reshape(shape), axis=0) / density
    speed_y = jnp.sum(stack * velocity_table[:, 1].reshape(shape), axis=0) / density
    speed_z = jnp.sum(stack * velocity_table[:, 2].reshape(shape), axis=0) / density
    return (density, speed_x, speed_y, speed_z)


def boost_face(face, components, change):
    density, speed_x, speed_y, speed_z = moments(face)
    result = []
    for component in components:
        east_step, north_step, upward_step = VELOCITIES[component]
        weight = WEIGHTS[component]
        projection = east_step * speed_x + north_step * speed_y + upward_step * speed_z
        shifted = projection + north_step * change
        square_old = speed_x * speed_x + speed_y * speed_y + speed_z * speed_z
        moved_y = speed_y + change
        square_new = speed_x * speed_x + moved_y * moved_y + speed_z * speed_z
        correction = (
            weight
            * density
            * (
                3.0 * (shifted - projection)
                + 4.5 * (shifted * shifted - projection * projection)
                - 1.5 * (square_new - square_old)
            )
        )
        result.append(face[component] + correction)
    return jnp.stack(result)


def collide(read, force_x, force_y, force_z):
    velocity_table = jnp.array(VELOCITIES, jnp.float32)
    shape = (19,) + (1,) * (read.ndim - 1)
    density = jnp.sum(read, axis=0)
    speed_x = (
        jnp.sum(read * velocity_table[:, 0].reshape(shape), axis=0) + 0.5 * force_x
    ) / density
    speed_y = (
        jnp.sum(read * velocity_table[:, 1].reshape(shape), axis=0) + 0.5 * force_y
    ) / density
    speed_z = (
        jnp.sum(read * velocity_table[:, 2].reshape(shape), axis=0) + 0.5 * force_z
    ) / density
    square = speed_x * speed_x + speed_y * speed_y + speed_z * speed_z
    outputs = []
    for component in range(19):
        east_step, north_step, upward_step = VELOCITIES[component]
        weight = WEIGHTS[component]
        projection = east_step * speed_x + north_step * speed_y + upward_step * speed_z
        balance = (
            weight
            * density
            * (1.0 + 3.0 * projection + 4.5 * projection * projection - 1.5 * square)
        )
        along_force = east_step * force_x + north_step * force_y + upward_step * force_z
        forcing = weight * (
            3.0
            * (
                (east_step - speed_x) * force_x
                + (north_step - speed_y) * force_y
                + (upward_step - speed_z) * force_z
            )
            + 9.0 * projection * along_force
        )
        outputs.append(
            read[component] - (read[component] - balance) / TAU + (1.0 - 0.5 / TAU) * forcing
        )
    return (jnp.stack(outputs), speed_x, speed_y, speed_z)


def laplace(values):
    center = values[1:-1, 1:-1]
    return (
        values[2:, 1:-1]
        + values[:-2, 1:-1]
        + values[1:-1, 2:]
        + values[1:-1, :-2]
        + jnp.roll(center, -1, 2)
        + jnp.roll(center, 1, 2)
        - 6.0 * center
    )


def gradient(values):
    center = values[1:-1, 1:-1]
    return (
        (values[2:, 1:-1] - values[:-2, 1:-1]) * 0.5,
        (values[1:-1, 2:] - values[1:-1, :-2]) * 0.5,
        (jnp.roll(center, -1, 2) - jnp.roll(center, 1, 2)) * 0.5,
    )


def per_device(
    populations,
    order_field,
    solid_flags,
    plane_flags,
    shear_shift,
    link_site,
    link_dir,
    link_colloid,
    link_count,
    colloid_slot,
    colloid_speed,
):
    slab_index = lax.axis_index("gx")
    slab_count = lax.axis_size("gx")
    pencil_index = lax.axis_index("gy")
    pencil_count = lax.axis_size("gy")
    slab_depth, pencil_width, column_height = order_field.shape
    total_rows = pencil_width * pencil_count
    plane_shift = shear_shift[0]
    plane_low = plane_flags[slab_index]
    plane_high = plane_flags[(slab_index + 1) % slab_count]
    low_offset = plane_shift * plane_low
    high_offset = plane_shift * plane_high
    low_face = populations[:, 0]
    high_face = populations[:, slab_depth - 1]
    down_plain = jnp.stack([low_face[component] for component in DOWN_X])
    up_plain = jnp.stack([high_face[component] for component in UP_X])
    down_going = jnp.where(plane_low == 1, boost_face(low_face, DOWN_X, PLANE_SPEED), down_plain)
    up_going = jnp.where(plane_high == 1, boost_face(high_face, UP_X, -PLANE_SPEED), up_plain)
    low_message = jnp.concatenate([down_going, order_field[0:2]], axis=0)
    high_message = jnp.concatenate([up_going, order_field[slab_depth - 2 : slab_depth]], axis=0)

    def window(gathered, first_row):
        doubled = jnp.concatenate([gathered, gathered], axis=1)
        begin = jnp.mod(first_row, total_rows)
        return lax.dynamic_slice_in_dim(doubled, begin, pencil_width + 4, 1)

    packed = jnp.stack([low_message, high_message], axis=1)
    arrived = padded_2(packed, (("gx", 1),), 1)
    incoming = jnp.stack([arrived[:, 0], arrived[:, 3]], axis=0)
    gathered = lax.all_gather(incoming, "gy", axis=2, tiled=True)
    below = window(gathered[0], pencil_index * pencil_width - 2 - low_offset)
    above = window(gathered[1], pencil_index * pencil_width - 2 + high_offset)
    low_rows = jnp.concatenate(
        [
            jnp.stack([populations[component, :, 0] for component in DOWN_Y]),
            order_field[None, :, 0],
            order_field[None, :, 1],
        ],
        axis=0,
    )
    high_rows = jnp.concatenate(
        [
            jnp.stack([populations[component, :, pencil_width - 1] for component in UP_Y]),
            order_field[None, :, pencil_width - 2],
            order_field[None, :, pencil_width - 1],
        ],
        axis=0,
    )
    rims = padded_2(jnp.stack([low_rows, high_rows], axis=2), (("gy", 2),), 1)
    from_below = rims[:, :, 0]
    from_above = rims[:, :, 3]
    middle = jnp.concatenate(
        [
            from_below[5][:, None],
            from_below[6][:, None],
            order_field,
            from_above[5][:, None],
            from_above[6][:, None],
        ],
        axis=1,
    )
    padded = jnp.concatenate(
        [below[5][None], below[6][None], middle, above[5][None], above[6][None]], axis=0
    )
    inner_order = padded[1:-1, 1:-1]
    potential = BULK * (inner_order * inner_order * inner_order - inner_order) - KAPPA * laplace(
        padded
    )
    slope_x, slope_y, slope_z = gradient(potential)
    phase_x, phase_y, phase_z = gradient(inner_order)
    potential_curve = laplace(potential)
    zero_row = jnp.zeros((slab_depth, 1, column_height), jnp.float32)
    zero_layer = jnp.zeros((1, pencil_width + 2, column_height), jnp.float32)
    pieces = []
    for component in range(19):
        east_step, north_step, upward_step = VELOCITIES[component]
        low_row = from_below[UP_Y.index(component)][:, None] if north_step == 1 else zero_row
        high_row = from_above[DOWN_Y.index(component)][:, None] if north_step == -1 else zero_row
        extended = jnp.concatenate([low_row, populations[component], high_row], axis=1)
        left_layer = (
            below[UP_X.index(component), 1 : pencil_width + 3][None]
            if east_step == 1
            else zero_layer
        )
        right_layer = (
            above[DOWN_X.index(component), 1 : pencil_width + 3][None]
            if east_step == -1
            else zero_layer
        )
        extended = jnp.concatenate([left_layer, extended, right_layer], axis=0)
        pulled = extended[
            1 - east_step : 1 - east_step + slab_depth,
            1 - north_step : 1 - north_step + pencil_width,
        ]
        pieces.append(jnp.roll(pulled, upward_step, 2))
    read = jnp.stack(pieces)
    velocity_table = jnp.array(VELOCITIES, jnp.float32)
    weight_table = jnp.array(WEIGHTS, jnp.float32)
    opposite_table = jnp.array(OPPOSITE, jnp.int32)
    flat_stream = read.reshape((19, -1))
    flat_post = populations.reshape((19, -1))
    position = jnp.arange(link_site.shape[0], dtype=jnp.int32)
    live_links = position % 128 < link_count[position // 128]
    source = flat_post[link_dir, link_site]
    direction_vec = velocity_table[link_dir]
    link_weight = weight_table[link_dir]
    link_speed = colloid_speed[:, link_colloid]
    projection = jnp.sum(direction_vec.T * link_speed, axis=0)
    returned = source - 6.0 * link_weight * projection
    target = opposite_table[link_dir]
    current = flat_stream[target, link_site]
    flat_stream = flat_stream.at[target, link_site].set(jnp.where(live_links, returned, current))
    read = flat_stream.reshape(read.shape)
    transfer = (
        jnp.where(live_links, 2.0 * source - 6.0 * link_weight * projection, 0.0) * direction_vec.T
    )
    partial_value = jax.ops.segment_sum(
        transfer.T, colloid_slot[link_colloid], num_segments=colloid_slot.shape[0]
    ).T
    colloid_force = lax.psum_scatter(partial_value, ("gx", "gy"), scatter_dimension=1, tiled=True)
    collided, speed_x, speed_y, speed_z = collide(
        read, -order_field * slope_x, -order_field * slope_y, -order_field * slope_z
    )
    solid_mask = solid_flags == 1
    weight_shape = weight_table.reshape((19, 1, 1, 1))
    new_populations = jnp.where(solid_mask[None], weight_shape + 0.0 * collided, collided)
    advanced = (
        order_field
        - (speed_x * phase_x + speed_y * phase_y + speed_z * phase_z)
        + MOBILITY * potential_curve
    )
    new_order = jnp.where(solid_mask, order_field, advanced)
    return (new_populations, new_order, colloid_force)


def solution(mesh):
    return jax.shard_map(
        per_device,
        mesh=mesh,
        in_specs=(
            P(None, "gx", "gy", None),
            P("gx", "gy", None),
            P("gx", "gy", None),
            P(),
            P(),
            P(("gx", "gy")),
            P(("gx", "gy")),
            P(("gx", "gy")),
            P(("gx", "gy")),
            P(),
            P(),
        ),
        out_specs=(P(None, "gx", "gy", None), P("gx", "gy", None), P(None, ("gx", "gy"))),
        check_vma=False,
    )
```

profile of v0, /device:TPU:1, one launch (start us, length us, event | category | flops | bytes accessed | tf_op | source)
XLA Modules:
  0.0 232.4 jit_solution(17619595374594204179)
XLA Ops:
  0.7 1.0 bitcast_reduce_fusion
  1.7 0.9 slice_reduce_fusion
  3.4 1.4 fusion.277
  5.4 1.1 fusion.4
  10.3 4.0 %collective-permute-start = (f32[7,1,16,128]{3,2,0,1:T(8,128)}, f32[7,1,16,128]{3,2,0,1:T(8,128)S(1)}, u32[]{:S(2)}, u32[]{:S(2)}) collective-permute-start(f32[7,1,16,128]{3,2,0,1:T(8,128)} %maximum_bitcast_fusion), channel_id=1, source_target_pairs={{0,4},{4,8},{8,12},{12,16},{16,20},{20,24},{24,28},{28,32},{32,36}... | collective-permute-start | bytes 172040 | tf_op jit(solution)/shard_map/ppermute | solution.py:46
  15.7 13.2 %collective-permute-start.1 = (f32[7,1,16,128]{3,2,0,1:T(8,128)}, f32[7,1,16,128]{3,2,0,1:T(8,128)}, u32[]{:S(2)}, u32[]{:S(2)}) collective-permute-start(f32[7,1,16,128]{3,2,0,1:T(8,128)} %maximum_bitcast_fusion.1), channel_id=1, source_target_pairs={{4,0},{8,4},{12,8},{16,12},{20,16},{24,20},{28,24},{32,28},{36,32}... | collective-permute-start | bytes 172040 | tf_op jit(solution)/shard_map/ppermute | solution.py:49
  33.1 5.2 %collective-permute-start.2 = (f32[7,8,1,128]{3,1,2,0:T(8,128)}, f32[7,8,1,128]{3,1,2,0:T(8,128)}, u32[]{:S(2)}, u32[]{:S(2)}) collective-permute-start(f32[7,8,1,128]{3,1,2,0:T(8,128)} %bitcast.45), channel_id=1, source_target_pairs={{0,1},{1,2},{2,3},{3,0},{4,5},{5,6},{6,7},{7,4},{8,9},{9,10},{10,1... | collective-permute-start | bytes 86024 | tf_op jit(solution)/shard_map/ppermute | solution.py:46
  42.4 1.9 collective-permute-start.3
  47.5 0.9 copy.154
  48.9 8.6 %gather_fusion = f32[1024]{0:T(1024)S(1)} fusion(f32[19,16384]{1,0:T(8,128)S(1)} %bitcast.664, s32[1024]{0:T(1024)S(1)} %bitcast.582), kind=kCustom, calls=%fused_computation | custom fusion | bytes 16384 | tf_op jit(solution)/shard_map/gather | solution.py:265
  57.5 2.8 %gather_fusion.2 = f32[1024,3]{1,0:T(8,128)S(1)} fusion(f32[3,2048]{0,1:T(8,128)S(1)} %copy.134, s32[1024]{0:T(1024)S(1)} %get-tuple-element.192), kind=kCustom, calls=%fused_computation.2 | custom fusion | bytes 28672 | tf_op jit(solution)/shard_map/gather | solution.py:268
  60.3 2.8 %gather_fusion.1 = f32[1024,3]{1,0:T(8,128)S(1)} fusion(f32[19,3]{1,0:T(8,128)S(1)} %copy-done.1, s32[1024]{0:T(1024)S(1)} %get-tuple-element.162), kind=kCustom, calls=%fused_computation.1 | custom fusion | bytes 28672 | tf_op jit(solution)/shard_map/gather | solution.py:266
  63.4 4.3 %compare_select_fusion.2 = s32[1024,1]{0,1:T(1,128)S(1)} fusion(s32[]{:T(128)} %bitcast.109, s32[]{:T(128)} %bitcast.110, s32[]{:T(128)} %bitcast.111, s32[]{:T(128)} %bitcast.112, s32[]{:T(128)} %bitcast.113, s32[]{:T(128)} %bitcast.115, s32[]{:T(128)} %bitcast.114), kind=kLoop, calls=%fused_computation.412 | loop fusion | flops 23552 | bytes 4124 | tf_op jit(solution)/shard_map/gather | solution.py:264
  67.7 1.2 subtract_select_fusion
  70.5 6.2 %gather_fusion.4 = s32[1024]{0:T(1024)S(1)} fusion(s32[2048]{0:T(1024)S(1)} %copy-done, s32[1024]{0:T(1024)S(1)} %get-tuple-element.192), kind=kCustom, calls=%fused_computation.4 | custom fusion | bytes 12288 | tf_op jit(solution)/shard_map/gather | solution.py:279
  76.7 6.8 %scatter_custom_fusion = f32[2048,3]{1,0:T(8,128)S(1)} fusion(s32[1024]{0:T(1024)S(1)} %gather_fusion.4, f32[1024,3]{1,0:T(8,128)S(1)} %gather_fusion.1, f32[]{:T(128)} %constant.148.clone.1, f32[1024]{0:T(1024)S(1)} %get-tuple-element.26), kind=kCustom, calls=%fused_computation.12 | custom fusion | flops 6144 | bytes 552964 | tf_op jit(solution)/shard_map/scatter-add | solution.py:278
  83.5 104.1 %all-reduce = f32[3,2048]{0,1:T(8,128)S(1)} all-reduce(f32[3,2048]{0,1:T(8,128)S(1)} %bitcast.667), channel_id=2, replica_groups=mesh['gx'=128,'gy'=4] {'gx','gy'}, use_global_device_ids=true, to_apply=%region_15.16.clone | all-reduce | flops 6144 | bytes 49152
  197.4 8.5 %all_gather.3 = f32[2,7,64,128]{3,2,1,0:T(8,128)S(1)} all-gather(f32[2,7,16,128]{3,2,1,0:T(8,128)S(1)} %pad_maximum_fusion.9), channel_id=1, replica_groups=mesh['gx'=128,'gy'=4] {'gy'}, dimensions={2}, use_global_device_ids=true | all-gather | bytes 573440 | tf_op jit(solution)/shard_map/all_gather | solution.py:191
  209.1 2.7 %stack.185 = f32[19,16384]{1,0:T(8,128)S(1)} concatenate(f32[1,16384]{1,0:T(1,128)S(1)} %bitcast.670, f32[1,16384]{1,0:T(1,128)S(1)} %bitcast.707, f32[1,16384]{1,0:T(1,128)S(1)} %bitcast.703, f32[1,16384]{1,0:T(1,128)} %bitcast.705, f32[1,16384]{1,0:T(1,128)} %bitcast.704, f32[1,16384]{1,0:T(1,128)S(1)} %bitcast.671, f32[1,16384]{1,0:T(1,128)S(1)} %bitcast.672, ...), dimensions={0} | concatenate | bytes 2490368 | tf_op jit(solution)/shard_map/stack | solution.py:257
  212.1 8.6 %gather_fusion.3 = f32[1024]{0:T(1024)S(1)} fusion(f32[19,16384]{1,0:T(8,128)S(1)} %stack.185, s32[1024]{0:T(1024)S(1)} %bitcast.583), kind=kCustom, calls=%fused_computation.3 | custom fusion | bytes 16384 | tf_op jit(solution)/shard_map/gather | solution.py:272
  220.7 5.0 %scatter_fusion = f32[311296]{0:T(1024)S(1)} fusion(f32[311296]{0:T(1024)S(1)} %reshape.949, s32[1024]{0:T(1024)S(1)} %copy-done.33, f32[1024]{0:T(1024)S(1)} %subtract_select_fusion.1), kind=kCustom, calls=%fused_computation.6 | custom fusion | bytes 16384
  226.7 1.0 multiply_reduce_fusion.1
  227.8 0.8 fusion.181
  231.1 1.2 add_select_fusion
  (208 shorter events, 32.9 us)
Async XLA Ops:
  0.6 69.9 %copy-start = (s32[2048]{0:T(1024)S(1)}, s32[2048]{0:T(1024)}, u32[]{:S(2)}) copy-start(s32[2048]{0:T(1024)} %param.26) | copy-start | bytes 24580
  0.6 8.9 %copy-start.2 = (f32[19,8,16,128]{3,2,1,0:T(8,128)S(1)}, f32[19,8,16,128]{3,2,1,0:T(8,128)}, u32[]{:S(2)}) copy-start(f32[19,8,16,128]{3,2,1,0:T(8,128)} %param.17) | copy-start | bytes 3735556
  0.7 28.3 %copy-start.3 = (f32[8,16,128]{2,1,0:T(8,128)S(1)}, f32[8,16,128]{2,1,0:T(8,128)}, u32[]{:S(2)}) copy-start(f32[8,16,128]{2,1,0:T(8,128)} %param.18) | copy-start | bytes 196612
  10.3 186.3 %collective-permute-start = (f32[7,1,16,128]{3,2,0,1:T(8,128)}, f32[7,1,16,128]{3,2,0,1:T(8,128)S(1)}, u32[]{:S(2)}, u32[]{:S(2)}) collective-permute-start(f32[7,1,16,128]{3,2,0,1:T(8,128)} %maximum_bitcast_fusion), channel_id=1, source_target_pairs={{0,4},{4,8},{8,12},{12,16},{16,20},{20,24},{24,28},{28,32},{32,36}... | collective-permute-start | bytes 172040 | tf_op jit(solution)/shard_map/ppermute | solution.py:46
  15.7 180.9 %collective-permute-start.1 = (f32[7,1,16,128]{3,2,0,1:T(8,128)}, f32[7,1,16,128]{3,2,0,1:T(8,128)}, u32[]{:S(2)}, u32[]{:S(2)}) collective-permute-start(f32[7,1,16,128]{3,2,0,1:T(8,128)} %maximum_bitcast_fusion.1), channel_id=1, source_target_pairs={{4,0},{8,4},{12,8},{16,12},{20,16},{24,20},{28,24},{32,28},{36,32}... | collective-permute-start | bytes 172040 | tf_op jit(solution)/shard_map/ppermute | solution.py:49
  33.1 158.0 %collective-permute-start.2 = (f32[7,8,1,128]{3,1,2,0:T(8,128)}, f32[7,8,1,128]{3,1,2,0:T(8,128)}, u32[]{:S(2)}, u32[]{:S(2)}) collective-permute-start(f32[7,8,1,128]{3,1,2,0:T(8,128)} %bitcast.45), channel_id=1, source_target_pairs={{0,1},{1,2},{2,3},{3,0},{4,5},{5,6},{6,7},{7,4},{8,9},{9,10},{10,1... | collective-permute-start | bytes 86024 | tf_op jit(solution)/shard_map/ppermute | solution.py:46
  42.4 149.4 %collective-permute-start.3 = (f32[7,8,1,128]{3,1,2,0:T(8,128)}, f32[7,8,1,128]{3,1,2,0:T(8,128)}, u32[]{:S(2)}, u32[]{:S(2)}) collective-permute-start(f32[7,8,1,128]{3,1,2,0:T(8,128)} %bitcast.58), channel_id=1, source_target_pairs={{1,0},{2,1},{3,2},{0,3},{5,4},{6,5},{7,6},{4,7},{9,8},{10,9},{11,1... | collective-permute-start | bytes 86024 | tf_op jit(solution)/shard_map/ppermute | solution.py:49
  44.4 2.3 copy-start.32
  44.4 2.9 %copy-start.38 = (s32[1024]{0:T(1024)S(1)}, s32[1024]{0:T(1024)}, u32[]{:S(2)}) copy-start(s32[1024]{0:T(1024)} %param.22) | copy-start | bytes 12292
  57.5 10.3 %copy-start.29 = (f32[1024]{0:T(1024)}, f32[1024]{0:T(1024)S(1)}, u32[]{:S(2)}) copy-start(f32[1024]{0:T(1024)S(1)} %gather_fusion) | copy-start | bytes 12292
  57.5 2.8 %copy-start.1 = (f32[19,3]{1,0:T(8,128)S(1)}, f32[19,3]{1,0:T(8,128)}, u32[]{:S(2)}) copy-start(f32[19,3]{1,0:T(8,128)} %constant.180.clone) | copy-start | bytes 688
  63.1 7.2 %copy-start.43 = (s32[2]{0:T(128)S(1)}, s32[2]{0:T(128)}, u32[]{:S(2)}) copy-start(s32[2]{0:T(128)} %constant.187) | copy-start | bytes 28
  63.1 7.3 %copy-start.42 = (s32[2]{0:T(128)S(1)}, s32[2]{0:T(128)}, u32[]{:S(2)}) copy-start(s32[2]{0:T(128)} %constant.190) | copy-start | bytes 28
  83.5 104.1 %copy-start.13 = (f32[8,16,1]{2,1,0:T(8,128)S(1)}, f32[8,16,1]{2,1,0:T(8,128)}, u32[]{:S(2)}) copy-start(f32[8,16,1]{2,1,0:T(8,128)} %slice.868) | copy-start | bytes 1540
  83.5 104.2 %copy-start.12 = (f32[8,16,127]{2,1,0:T(8,128)S(1)}, f32[8,16,127]{2,1,0:T(8,128)}, u32[]{:S(2)}) copy-start(f32[8,16,127]{2,1,0:T(8,128)} %slice.870) | copy-start | bytes 195076
  187.6 7.5 %copy-start.20 = (f32[8,16,128]{2,1,0:T(8,128)S(1)}, f32[8,16,128]{2,1,0:T(8,128)}, u32[]{:S(2)}) copy-start(f32[8,16,128]{2,1,0:T(8,128)} %get-tuple-element.81) | copy-start | bytes 196612
  187.6 7.5 %copy-start.21 = (f32[8,16,128]{2,1,0:T(8,128)S(1)}, f32[8,16,128]{2,1,0:T(8,128)}, u32[]{:S(2)}) copy-start(f32[8,16,128]{2,1,0:T(8,128)} %get-tuple-element.82) | copy-start | bytes 196612
  192.5 13.3 %copy-start.27 = (f32[1,8,1,128]{3,1,2,0:T(8,128)}, f32[1,8,1,128]{3,1,2,0:T(8,128)S(1)}, u32[]{:S(2)}) copy-start(f32[1,8,1,128]{3,1,2,0:T(8,128)S(1)} %get-tuple-element.147) | copy-start | bytes 12292
  206.2 1.7 copy-start.4
  206.2 1.7 copy-start.5
  212.0 8.6 %copy-start.30 = (f32[1024]{0:T(1024)S(1)}, f32[1024]{0:T(1024)}, u32[]{:S(2)}) copy-start(f32[1024]{0:T(1024)} %copy-done.29) | copy-start | bytes 12292
  212.1 8.6 %copy-start.35 = (f32[1024]{0:T(1024)S(1)}, f32[1024]{0:T(1024)}, u32[]{:S(2)}) copy-start(f32[1024]{0:T(1024)} %get-tuple-element.27) | copy-start | bytes 12292
  212.1 8.6 %copy-start.37 = (pred[1024]{0:T(1024)(128)(4,1)S(1)}, pred[1024]{0:T(1024)(128)(4,1)}, u32[]{:S(2)}) copy-start(pred[1024]{0:T(1024)(128)(4,1)} %get-tuple-element.28) | copy-start | bytes 3076
  212.1 8.7 %copy-start.33 = (s32[1024]{0:T(1024)S(1)}, s32[1024]{0:T(1024)}, u32[]{:S(2)}) copy-start(s32[1024]{0:T(1024)} %broadcast_select_fusion.2) | copy-start | bytes 12292
  (25 other events, 25.8 us)
where the time goes:
time: 233 us; the launch traced here: 232 us
  blocking collectives  113 us (48%)
  local copies, waits for them, and re-layouts  58.8 us (25%)
  other arithmetic  31.5 us (14%)
  starting transfers between devices  24.3 us (10%)
  between operations  5.2 us (2%)
    unnamed x1, blocking collectives  104 us
    unnamed x112, local copies, waits for them, and re-layouts  15.5 us
    ppermute x2, starting transfers between devices, padded_2(): lax.ppermute(lax.slice_in_dim(block, 0, width, axis=dim), axis, backward)  15.1 us
    ppermute x2, starting transfers between devices, padded_2(): lax.ppermute(lax.slice_in_dim(block, block.shape[dim] - width, None, axis...  9.21 us
    gather x1, local copies, waits for them, and re-layouts, per_device(): source = flat_post[link_dir, link_site]  8.59 us
    gather x1, local copies, waits for them, and re-layouts, per_device(): current = flat_stream[target, link_site]  8.59 us
    all_gather x1, blocking collectives, per_device(): gathered = lax.all_gather(incoming, 'gy', axis=2, tiled=True)  8.5 us
    scatter-add x1, other arithmetic, per_device(): jax.ops.segment_sum(transfer.T, colloid_slot[link_colloid], num_segments=...  6.8 us
  transfers between devices with their start and end apart: 4, of which 0 were waited for; matrix products, arithmetic and copies ran while one was open for 24% of the time, Pallas kernels for 0%

commit v1 on v0

--- a/solution.py
+++ b/solution.py
@@ -188,7 +188,8 @@
     packed = jnp.stack([low_message, high_message], axis=1)
     arrived = padded_2(packed, (("gx", 1),), 1)
     incoming = jnp.stack([arrived[:, 0], arrived[:, 3]], axis=0)
-    gathered = lax.all_gather(incoming, "gy", axis=2, tiled=True)
+    sent = jnp.stack([incoming] * lax.axis_size("gy"))
+    gathered = jnp.concatenate(lax.all_to_all(sent, "gy", 0, 0), axis=2)
     below = window(gathered[0], pencil_index * pencil_width - 2 - low_offset)
     above = window(gathered[1], pencil_index * pencil_width - 2 + high_offset)
     low_rows = jnp.concatenate(

time: 233 us -> 235 us (level)
  blocking collectives: 113 us -> 104 us
  waiting for transfers between devices: 0.01 us -> 6.38 us
  starting transfers between devices: 24.3 us -> 28.6 us
    all_gather x1 -> x0, blocking collectives: 8.5 us -> none  [per_device(): gathered = lax.all_gather(incoming, 'gy', axis=2, tiled=True)]
    all_to_all x0 -> x1, waiting for transfers between devices: none -> 6.37 us  [per_device(): gathered = jnp.concatenate(lax.all_to_all(sent, 'gy', 0, 0), axis=2)]
    all_to_all x0 -> x1, starting transfers between devices: none -> 4.28 us  [per_device(): gathered = jnp.concatenate(lax.all_to_all(sent, 'gy', 0, 0), axis=2)]
    unnamed x112 -> x108, local copies, waits for them, and re-layouts: 15.5 us -> 15.4 us
  transfers between devices with their start and end apart: 4 -> 5, of which waited for: 0 -> 1; matrix products, arithmetic and copies ran while one was open for 24% -> 23% of each run, Pallas kernels for 0% -> 0%
where the time goes in v1:
time: 235 us; the launch traced here: 234 us
  blocking collectives  104 us (44%)
  local copies, waits for them, and re-layouts  59.5 us (25%)
  other arithmetic  30.4 us (13%)
  starting transfers between devices  28.6 us (12%)
  waiting for transfers between devices  6.38 us (3%)
  between operations  4.94 us (2%)
    unnamed x1, blocking collectives  104 us
    unnamed x108, local copies, waits for them, and re-layouts  15.4 us
    ppermute x2, starting transfers between devices, padded_2(): lax.ppermute(lax.slice_in_dim(block, 0, width, axis=dim), axis, backward)  15.1 us
    ppermute x2, starting transfers between devices, padded_2(): lax.ppermute(lax.slice_in_dim(block, block.shape[dim] - width, None, axis...  9.21 us
    gather x1, local copies, waits for them, and re-layouts, per_device(): source = flat_post[link_dir, link_site]  8.59 us
    gather x1, local copies, waits for them, and re-layouts, per_device(): current = flat_stream[target, link_site]  8.59 us
    scatter-add x1, other arithmetic, per_device(): jax.ops.segment_sum(transfer.T, colloid_slot[link_colloid], num_segments=...  6.8 us
    all_to_all x1, waiting for transfers between devices, per_device(): gathered = jnp.concatenate(lax.all_to_all(sent, 'gy', 0, 0), axis=2)  6.37 us
  transfers between devices with their start and end apart: 5, of which 1 were waited for; matrix products, arithmetic and copies ran while one was open for 23% of the time, Pallas kernels for 0%

profile of v1, /device:TPU:1, one launch (start us, length us, event | category | flops | bytes accessed | tf_op | source)
XLA Modules:
  0.0 233.9 jit_solution(934361544118235824)
XLA Ops:
  0.7 1.0 bitcast_reduce_fusion
  1.7 0.9 slice_reduce_fusion
  3.4 1.3 fusion.278
  5.4 1.1 fusion.4
  10.2 4.0 %collective-permute-start = (f32[7,1,16,128]{3,2,0,1:T(8,128)}, f32[7,1,16,128]{3,2,0,1:T(8,128)S(1)}, u32[]{:S(2)}, u32[]{:S(2)}) collective-permute-start(f32[7,1,16,128]{3,2,0,1:T(8,128)} %maximum_bitcast_fusion), channel_id=1, source_target_pairs={{0,4},{4,8},{8,12},{12,16},{16,20},{20,24},{24,28},{28,32},{32,36}... | collective-permute-start | bytes 172040 | tf_op jit(solution)/shard_map/ppermute | solution.py:46
  15.5 13.2 %collective-permute-start.1 = (f32[7,1,16,128]{3,2,0,1:T(8,128)}, f32[7,1,16,128]{3,2,0,1:T(8,128)}, u32[]{:S(2)}, u32[]{:S(2)}) collective-permute-start(f32[7,1,16,128]{3,2,0,1:T(8,128)} %maximum_bitcast_fusion.1), channel_id=1, source_target_pairs={{4,0},{8,4},{12,8},{16,12},{20,16},{24,20},{28,24},{32,28},{36,32}... | collective-permute-start | bytes 172040 | tf_op jit(solution)/shard_map/ppermute | solution.py:49
  32.9 5.2 %collective-permute-start.2 = (f32[7,8,1,128]{3,1,2,0:T(8,128)}, f32[7,8,1,128]{3,1,2,0:T(8,128)}, u32[]{:S(2)}, u32[]{:S(2)}) collective-permute-start(f32[7,8,1,128]{3,1,2,0:T(8,128)} %bitcast.46), channel_id=1, source_target_pairs={{0,1},{1,2},{2,3},{3,0},{4,5},{5,6},{6,7},{7,4},{8,9},{9,10},{10,1... | collective-permute-start | bytes 86024 | tf_op jit(solution)/shard_map/ppermute | solution.py:46
  42.2 1.9 collective-permute-start.3
  47.3 0.9 copy.186
  48.6 8.6 %gather_fusion = f32[1024]{0:T(1024)S(1)} fusion(f32[19,16384]{1,0:T(8,128)S(1)} %bitcast.665, s32[1024]{0:T(1024)S(1)} %bitcast.583), kind=kCustom, calls=%fused_computation | custom fusion | bytes 16384 | tf_op jit(solution)/shard_map/gather | solution.py:266
  57.3 2.8 %gather_fusion.2 = f32[1024,3]{1,0:T(8,128)S(1)} fusion(f32[3,2048]{0,1:T(8,128)S(1)} %copy.166, s32[1024]{0:T(1024)S(1)} %get-tuple-element.198), kind=kCustom, calls=%fused_computation.2 | custom fusion | bytes 28672 | tf_op jit(solution)/shard_map/gather | solution.py:269
  60.1 2.8 %gather_fusion.1 = f32[1024,3]{1,0:T(8,128)S(1)} fusion(f32[19,3]{1,0:T(8,128)S(1)} %copy-done.1, s32[1024]{0:T(1024)S(1)} %get-tuple-element.165), kind=kCustom, calls=%fused_computation.1 | custom fusion | bytes 28672 | tf_op jit(solution)/shard_map/gather | solution.py:267
  63.1 4.4 %compare_select_fusion.2 = s32[1024,1]{0,1:T(1,128)S(1)} fusion(s32[]{:T(128)} %bitcast.110, s32[]{:T(128)} %bitcast.111, s32[]{:T(128)} %bitcast.112, s32[]{:T(128)} %bitcast.113, s32[]{:T(128)} %bitcast.114, s32[]{:T(128)} %bitcast.116, s32[]{:T(128)} %bitcast.115), kind=kLoop, calls=%fused_computation.411 | loop fusion | flops 23552 | bytes 4124 | tf_op jit(solution)/shard_map/gather | solution.py:265
  67.5 1.3 subtract_select_fusion
  70.5 6.2 %gather_fusion.4 = s32[1024]{0:T(1024)S(1)} fusion(s32[2048]{0:T(1024)S(1)} %copy-done, s32[1024]{0:T(1024)S(1)} %get-tuple-element.198), kind=kCustom, calls=%fused_computation.4 | custom fusion | bytes 12288 | tf_op jit(solution)/shard_map/gather | solution.py:280
  76.6 6.8 %scatter_custom_fusion = f32[2048,3]{1,0:T(8,128)S(1)} fusion(s32[1024]{0:T(1024)S(1)} %gather_fusion.4, f32[1024,3]{1,0:T(8,128)S(1)} %gather_fusion.1, f32[]{:T(128)} %constant.148.clone.1, f32[1024]{0:T(1024)S(1)} %get-tuple-element.29), kind=kCustom, calls=%fused_computation.12 | custom fusion | flops 6144 | bytes 552964 | tf_op jit(solution)/shard_map/scatter-add | solution.py:279
  83.5 104.1 %all-reduce = f32[3,2048]{0,1:T(8,128)S(1)} all-reduce(f32[3,2048]{0,1:T(8,128)S(1)} %bitcast.668), channel_id=2, replica_groups=mesh['gx'=128,'gy'=4] {'gx','gy'}, use_global_device_ids=true, to_apply=%region_15.16.clone | all-reduce | flops 6144 | bytes 49152
  194.4 4.3 %all-to-all-start = ((f32[4,2,7,16,128]{4,3,2,1,0:T(8,128)}), f32[4,2,7,16,128]{4,3,2,1,0:T(8,128)S(1)}, u32[]{:S(2)}, u32[]{:S(2)}) async-start(f32[4,2,7,16,128]{4,3,2,1,0:T(8,128)} %stack.172), calls=%async_computation | async-start | bytes 917504 | tf_op jit(solution)/shard_map/all_to_all | solution.py:192
  201.1 6.4 %all-to-all-done = f32[4,2,7,16,128]{4,3,2,1,0:T(8,128)S(1)} async-done(((f32[4,2,7,16,128]{4,3,2,1,0:T(8,128)}), f32[4,2,7,16,128]{4,3,2,1,0:T(8,128)S(1)}, u32[]{:S(2)}, u32[]{:S(2)}) %all-to-all-start) | async-done | bytes 458784 | tf_op jit(solution)/shard_map/all_to_all | solution.py:192
  210.6 2.7 %stack.193 = f32[19,16384]{1,0:T(8,128)S(1)} concatenate(f32[1,16384]{1,0:T(1,128)S(1)} %bitcast.674, f32[1,16384]{1,0:T(1,128)S(1)} %bitcast.711, f32[1,16384]{1,0:T(1,128)S(1)} %bitcast.707, f32[1,16384]{1,0:T(1,128)} %bitcast.709, f32[1,16384]{1,0:T(1,128)} %bitcast.708, f32[1,16384]{1,0:T(1,128)S(1)} %bitcast.675, f32[1,16384]{1,0:T(1,128)S(1)} %bitcast.676, ...), dimensions={0} | concatenate | bytes 2490368 | tf_op jit(solution)/shard_map/stack | solution.py:258
  213.6 8.6 %gather_fusion.3 = f32[1024]{0:T(1024)S(1)} fusion(f32[19,16384]{1,0:T(8,128)S(1)} %stack.193, s32[1024]{0:T(1024)S(1)} %bitcast.584), kind=kCustom, calls=%fused_computation.3 | custom fusion | bytes 16384 | tf_op jit(solution)/shard_map/gather | solution.py:273
  222.3 5.0 %scatter_fusion = f32[311296]{0:T(1024)S(1)} fusion(f32[311296]{0:T(1024)S(1)} %reshape.960, s32[1024]{0:T(1024)S(1)} %copy-done.31, f32[1024]{0:T(1024)S(1)} %subtract_select_fusion.1), kind=kCustom, calls=%fused_computation.6 | custom fusion | bytes 16384
  228.3 1.0 multiply_reduce_fusion.1
  232.7 1.2 add_select_fusion
  (207 shorter events, 33.3 us)
Async XLA Ops:
  0.6 69.8 %copy-start = (s32[2048]{0:T(1024)S(1)}, s32[2048]{0:T(1024)}, u32[]{:S(2)}) copy-start(s32[2048]{0:T(1024)} %param.26) | copy-start | bytes 24580
  0.6 8.9 %copy-start.2 = (f32[19,8,16,128]{3,2,1,0:T(8,128)S(1)}, f32[19,8,16,128]{3,2,1,0:T(8,128)}, u32[]{:S(2)}) copy-start(f32[19,8,16,128]{3,2,1,0:T(8,128)} %param.17) | copy-start | bytes 3735556
  0.7 28.1 %copy-start.3 = (f32[8,16,128]{2,1,0:T(8,128)S(1)}, f32[8,16,128]{2,1,0:T(8,128)}, u32[]{:S(2)}) copy-start(f32[8,16,128]{2,1,0:T(8,128)} %param.18) | copy-start | bytes 196612
  10.2 182.5 %collective-permute-start = (f32[7,1,16,128]{3,2,0,1:T(8,128)}, f32[7,1,16,128]{3,2,0,1:T(8,128)S(1)}, u32[]{:S(2)}, u32[]{:S(2)}) collective-permute-start(f32[7,1,16,128]{3,2,0,1:T(8,128)} %maximum_bitcast_fusion), channel_id=1, source_target_pairs={{0,4},{4,8},{8,12},{12,16},{16,20},{20,24},{24,28},{28,32},{32,36}... | collective-permute-start | bytes 172040 | tf_op jit(solution)/shard_map/ppermute | solution.py:46
  15.5 177.2 %collective-permute-start.1 = (f32[7,1,16,128]{3,2,0,1:T(8,128)}, f32[7,1,16,128]{3,2,0,1:T(8,128)}, u32[]{:S(2)}, u32[]{:S(2)}) collective-permute-start(f32[7,1,16,128]{3,2,0,1:T(8,128)} %maximum_bitcast_fusion.1), channel_id=1, source_target_pairs={{4,0},{8,4},{12,8},{16,12},{20,16},{24,20},{28,24},{32,28},{36,32}... | collective-permute-start | bytes 172040 | tf_op jit(solution)/shard_map/ppermute | solution.py:49
  32.9 158.0 %collective-permute-start.2 = (f32[7,8,1,128]{3,1,2,0:T(8,128)}, f32[7,8,1,128]{3,1,2,0:T(8,128)}, u32[]{:S(2)}, u32[]{:S(2)}) collective-permute-start(f32[7,8,1,128]{3,1,2,0:T(8,128)} %bitcast.46), channel_id=1, source_target_pairs={{0,1},{1,2},{2,3},{3,0},{4,5},{5,6},{6,7},{7,4},{8,9},{9,10},{10,1... | collective-permute-start | bytes 86024 | tf_op jit(solution)/shard_map/ppermute | solution.py:46
  42.2 149.4 %collective-permute-start.3 = (f32[7,8,1,128]{3,1,2,0:T(8,128)}, f32[7,8,1,128]{3,1,2,0:T(8,128)}, u32[]{:S(2)}, u32[]{:S(2)}) collective-permute-start(f32[7,8,1,128]{3,1,2,0:T(8,128)} %bitcast.59), channel_id=1, source_target_pairs={{1,0},{2,1},{3,2},{0,3},{5,4},{6,5},{7,6},{4,7},{9,8},{10,9},{11,1... | collective-permute-start | bytes 86024 | tf_op jit(solution)/shard_map/ppermute | solution.py:49
  44.2 2.2 copy-start.30
  44.2 2.9 %copy-start.36 = (s32[1024]{0:T(1024)S(1)}, s32[1024]{0:T(1024)}, u32[]{:S(2)}) copy-start(s32[1024]{0:T(1024)} %param.22) | copy-start | bytes 12292
  57.2 10.3 %copy-start.27 = (f32[1024]{0:T(1024)}, f32[1024]{0:T(1024)S(1)}, u32[]{:S(2)}) copy-start(f32[1024]{0:T(1024)S(1)} %gather_fusion) | copy-start | bytes 12292
  57.2 2.8 %copy-start.1 = (f32[19,3]{1,0:T(8,128)S(1)}, f32[19,3]{1,0:T(8,128)}, u32[]{:S(2)}) copy-start(f32[19,3]{1,0:T(8,128)} %constant.180.clone) | copy-start | bytes 688
  62.9 7.4 %copy-start.41 = (s32[2]{0:T(128)S(1)}, s32[2]{0:T(128)}, u32[]{:S(2)}) copy-start(s32[2]{0:T(128)} %constant.187) | copy-start | bytes 28
  62.9 7.4 %copy-start.40 = (s32[2]{0:T(128)S(1)}, s32[2]{0:T(128)}, u32[]{:S(2)}) copy-start(s32[2]{0:T(128)} %constant.190) | copy-start | bytes 28
  83.4 104.1 %copy-start.11 = (f32[8,16,1]{2,1,0:T(8,128)S(1)}, f32[8,16,1]{2,1,0:T(8,128)}, u32[]{:S(2)}) copy-start(f32[8,16,1]{2,1,0:T(8,128)} %slice.870) | copy-start | bytes 1540
  83.4 104.2 %copy-start.10 = (f32[8,16,127]{2,1,0:T(8,128)S(1)}, f32[8,16,127]{2,1,0:T(8,128)}, u32[]{:S(2)}) copy-start(f32[8,16,127]{2,1,0:T(8,128)} %slice.872) | copy-start | bytes 195076
  192.3 6.4 %copy-start.25 = (f32[1,8,1,128]{3,1,2,0:T(8,128)}, f32[1,8,1,128]{3,1,2,0:T(8,128)S(1)}, u32[]{:S(2)}) copy-start(f32[1,8,1,128]{3,1,2,0:T(8,128)S(1)} %get-tuple-element.150) | copy-start | bytes 12292
  192.7 7.7 %copy-start.18 = (f32[8,16,128]{2,1,0:T(8,128)S(1)}, f32[8,16,128]{2,1,0:T(8,128)}, u32[]{:S(2)}) copy-start(f32[8,16,128]{2,1,0:T(8,128)} %get-tuple-element.84) | copy-start | bytes 196612
  192.7 7.7 %copy-start.19 = (f32[8,16,128]{2,1,0:T(8,128)S(1)}, f32[8,16,128]{2,1,0:T(8,128)}, u32[]{:S(2)}) copy-start(f32[8,16,128]{2,1,0:T(8,128)} %get-tuple-element.85) | copy-start | bytes 196612
  194.4 13.1 %all-to-all-start = ((f32[4,2,7,16,128]{4,3,2,1,0:T(8,128)}), f32[4,2,7,16,128]{4,3,2,1,0:T(8,128)S(1)}, u32[]{:S(2)}, u32[]{:S(2)}) async-start(f32[4,2,7,16,128]{4,3,2,1,0:T(8,128)} %stack.172), calls=%async_computation | async-start | bytes 917504 | tf_op jit(solution)/shard_map/all_to_all | solution.py:192
  207.8 1.7 copy-start.4
  213.6 8.6 %copy-start.28 = (f32[1024]{0:T(1024)S(1)}, f32[1024]{0:T(1024)}, u32[]{:S(2)}) copy-start(f32[1024]{0:T(1024)} %copy-done.27) | copy-start | bytes 12292
  213.6 8.6 %copy-start.33 = (f32[1024]{0:T(1024)S(1)}, f32[1024]{0:T(1024)}, u32[]{:S(2)}) copy-start(f32[1024]{0:T(1024)} %get-tuple-element.30) | copy-start | bytes 12292
  213.6 8.6 %copy-start.35 = (pred[1024]{0:T(1024)(128)(4,1)S(1)}, pred[1024]{0:T(1024)(128)(4,1)}, u32[]{:S(2)}) copy-start(pred[1024]{0:T(1024)(128)(4,1)} %get-tuple-element.31) | copy-start | bytes 3076
  213.6 8.7 %copy-start.31 = (s32[1024]{0:T(1024)S(1)}, s32[1024]{0:T(1024)}, u32[]{:S(2)}) copy-start(s32[1024]{0:T(1024)} %broadcast_select_fusion.2) | copy-start | bytes 12292
  (24 other events, 25.7 us)
